TPU v7x, 512 devices: a whole 4x8x8 slice. The times are simulated.
512 devices in a mesh: dp: 32 (over x, y), table: 16 (over z, core).
Axes of the slice: x: 4, y: 8, z: 8, core: 2. Of those that a mesh axis runs over, the one named last changes fastest.
Arguments:
- table: bfloat16 [12288, 512], P('table'), may hold values from -6 to 6
- history_shard: int32 [512, 256, 1], P(('dp', 'table')), may hold values from 0 to 15; in each aligned block of 256 rows (0 to 255, 256 to 511, ..., all dimensions but the last counted through in order) at most 32 rows name the same one
- history_row: int32 [512, 256], P(('dp', 'table')), may hold values from 0 to 767
- lengths: int32 [512], P(('dp', 'table')), may hold values from 1 to 256, 98304 in all
- w_in: bfloat16 [512, 2048], replicated, may hold values from -0.25 to 0.25
- w_out: bfloat16 [512, 512], replicated, may hold values from -0.25 to 0.25
- cotangent: bfloat16 [512, 256, 512], P(('dp', 'table')), may hold values from -6 to 6
Outputs:
- table_grad: float32 [12288, 512], P('table')
- dense_grad: bfloat16 [512, 512], replicated
Inputs may be any that keep to these rules, and one draw needn't show every extreme that they name: `history_shard`: among the 256 history slots of one device's samples, at most 32 name one table shard, and that bound is met by some shard in some device's slots. `lengths`: some sample has the full length 256.
All inputs are finite; a program needn't handle non-finite values. No bound on the sum of `lengths` on one device may be relied on, other than what follows from the above.
Results may differ from a plain program's by a relative error of at most 0.017.
Values may be sent and summed in bfloat16 or wider, within the bound.
A program may use at most 64 MiB of HBM per device.

v0:
```python
import math
import jax
import jax.numpy as jnp
from jax import lax
from jax.sharding import PartitionSpec as P

HEADS = 4


def layer_norm(values):
    average = jnp.mean(values, axis=-1, keepdims=True)
    centred = values - average
    variance = jnp.mean(centred * centred, axis=-1, keepdims=True)
    return centred * lax.rsqrt(variance + 1e-06)


def hstu_layer(embedded, w_in, w_out, lengths):
    samples_here, seq_span, model_width = embedded.shape
    head_dim = model_width // HEADS
    normed = layer_norm(embedded.astype(jnp.float32)).astype(jnp.bfloat16)
    projected = jax.nn.silu(
        jnp.dot(
            normed.reshape(samples_here * seq_span, model_width),
            w_in,
            preferred_element_type=jnp.float32,
        )
    )
    gate_part = projected[:, :model_width]
    shaped = (samples_here, seq_span, HEADS, head_dim)
    values = projected[:, model_width : 2 * model_width].astype(jnp.bfloat16).reshape(shaped)
    queries = projected[:, 2 * model_width : 3 * model_width].astype(jnp.bfloat16).reshape(shaped)
    keys = projected[:, 3 * model_width :].astype(jnp.bfloat16).reshape(shaped)
    scores = jnp.einsum(
        "blhd,bmhd->bhlm", queries.astype(jnp.float32), keys.astype(jnp.float32)
    ) * head_dim ** (-0.5)
    positions = jnp.arange(seq_span)
    live_keys = (positions[None, None, :] <= positions[None, :, None]) & (
        positions[None, None, :] < lengths[:, None, None]
    )
    weights = (
        jnp.where(live_keys[:, None], jax.nn.silu(scores), 0.0)
        / lengths.astype(jnp.float32)[:, None, None, None]
    )
    weights = weights.astype(jnp.bfloat16)
    attended = jnp.einsum(
        "bhlm,bmhd->blhd", weights.astype(jnp.float32), values.astype(jnp.float32)
    ).reshape(samples_here * seq_span, model_width)
    mixed = (layer_norm(attended) * gate_part).astype(jnp.bfloat16)
    output = jnp.dot(mixed, w_out, preferred_element_type=jnp.float32) + embedded.reshape(
        -1, model_width
    ).astype(jnp.float32)
    return (output, mixed)


def per_device(table, history_shard, history_row, lengths, w_in, w_out, cotangent):
    shard_rows, model_width = table.shape
    samples_here, seq_span = history_row.shape
    groups = lax.axis_size("table")
    slot_count = samples_here * seq_span
    capacity = 2 * slot_count // groups
    owners = history_shard[:, :, 0].reshape(-1)
    local_rows = history_row.reshape(-1)
    owner_hits = (owners[:, None] == jnp.arange(groups)[None, :]).astype(jnp.int32)
    slot_rank = jnp.sum((jnp.cumsum(owner_hits, axis=0) - owner_hits) * owner_hits, axis=1)
    position = owners * capacity + slot_rank
    requested = (
        jnp.zeros((groups * capacity,), jnp.int32)
        .at[position]
        .set(local_rows)
        .reshape(groups, capacity)
    )
    incoming = lax.all_to_all(requested, "table", split_axis=0, concat_axis=0, tiled=True).reshape(
        -1
    )
    global_rows = owners * shard_rows + local_rows
    piece = lax.all_gather(table, "table", axis=0, tiled=True)
    inside = (global_rows >= 0) & (global_rows < piece.shape[0])
    taken = piece[jnp.clip(global_rows, 0, piece.shape[0] - 1)].astype(jnp.float32)
    embedded = jnp.where(inside[:, None], taken, 0.0).astype(jnp.bfloat16)
    embedded = embedded.reshape(samples_here, seq_span, model_width)
    output, pullback, mixed = jax.vjp(
        lambda rows_in: hstu_layer(rows_in, w_in, w_out, lengths), embedded, has_aux=True
    )
    row_live = jnp.arange(seq_span)[None, :] < lengths[:, None]
    grad_seed = jnp.where(row_live[:, :, None], cotangent, jnp.zeros_like(cotangent))
    flat_seed = grad_seed.reshape(-1, model_width)
    (row_grad,) = pullback(flat_seed.astype(jnp.float32))
    dense_part = jnp.dot(mixed.T, flat_seed, preferred_element_type=jnp.float32)
    outgoing = (
        jnp.zeros((groups * capacity, model_width), jnp.bfloat16)
        .at[position]
        .set(row_grad.reshape(-1, model_width))
    )
    arrived = lax.all_to_all(
        outgoing.reshape(groups, capacity, model_width),
        "table",
        split_axis=0,
        concat_axis=0,
        tiled=True,
    )
    local_grad = (
        jnp.zeros((shard_rows, model_width), jnp.float32)
        .at[incoming]
        .add(arrived.reshape(-1, model_width).astype(jnp.float32))
    )
    total_slots = slot_count * lax.axis_size("dp") * groups
    grad_scale = 1.0 / math.sqrt(total_slots)
    table_grad = lax.psum(local_grad, "dp")
    dense_total = lax.psum(dense_part, ("dp", "table"))
    dense_grad = (dense_total * grad_scale).astype(jnp.bfloat16)
    return (table_grad, dense_grad)


def solution(mesh):
    in_specs = (
        P("table", None),
        P(("dp", "table"), None, None),
        P(("dp", "table"), None),
        P(("dp", "table")),
        P(),
        P(),
        P(("dp", "table"), None, None),
    )
    out_specs = (P("table", None), P())
    return jax.shard_map(
        per_device, mesh=mesh, in_specs=in_specs, out_specs=out_specs, check_vma=False
    )
```

profile of v0, /device:TPU:64, one launch (start us, length us, event | category | flops | bytes accessed | tf_op | source)
XLA Modules:
  0.0 582.9 jit_solution(10138484838293075610)
XLA Ops:
  7.2 0.7 all-gather.2.cloned.1.call-update
  7.9 0.7 fusion.64
  9.4 0.8 fusion.63
  10.2 0.7 compare_select_fusion.1
  10.9 1.6 scatter_custom_fusion
  12.4 0.7 all_to_all.9
  13.1 10.0 %all-to-all-start = ((s32[16,1,32]{2,1,0:T(1,128)}), s32[16,1,32]{2,1,0:T(1,128)S(1)}, u32[]{:S(2)}, u32[]{:S(2)}) async-start(s32[16,1,32]{2,1,0:T(1,128)} %all_to_all.9), calls=%async_computation | async-start | bytes 16384 | tf_op jit(solution)/shard_map/all_to_all | solution.py:72
  23.8 0.7 compare_and_fusion
  24.5 66.3 %all-gather.2.cloned.1.call-done = bf16[12288,512]{1,0:T(8,128)(2,1)} async-done(((bf16[768,512]{1,0:T(8,128)(2,1)}), bf16[12288,512]{1,0:T(8,128)(2,1)}) %all-gather.2.cloned.1.call-update) | async-done | bytes 12582928 | tf_op jit(solution)/shard_map/all_gather | solution.py:76
  90.8 7.4 %gather_fusion = bf16[256,512]{1,0:T(8,128)(2,1)S(1)} fusion(bf16[12288,512]{1,0:T(8,128)(2,1)} %all-gather.2.cloned.1.call-done, s32[1024]{0:T(1024)S(1)} %pad_clamp_fusion), kind=kCustom, calls=%fused_computation | custom fusion | bytes 525312 | tf_op jit(solution)/shard_map/gather | solution.py:78
  98.7 2.8 fusion.76
  101.5 0.8 slice_bitcast_fusion
  102.5 1.6 divide_convert_fusion
  105.1 1.7 multiply_reduce_fusion.1
  106.9 2.1 fusion.75
  109.2 2.0 fusion.26
  111.5 1.0 fusion.79
  112.5 0.9 fusion.81
  113.6 1.8 copy.38
  115.4 1.8 copy.39
  117.2 3.4 multiply_reduce_fusion
  120.6 1.0 fusion.74
  121.6 2.9 scatter_custom_fusion.1
  124.5 6.9 %all-to-all-start.1 = ((bf16[16,32,512]{2,1,0:T(8,128)(2,1)}), bf16[16,32,512]{2,1,0:T(8,128)(2,1)}, u32[]{:S(2)}, u32[]{:S(2)}) async-start(bf16[16,32,512]{2,1,0:T(8,128)(2,1)} %bitcast.120), calls=%async_computation.1 | async-start | bytes 1048576 | tf_op jit(solution)/shard_map/all_to_all | solution.py:94
  131.6 2.5 fusion.45
  134.7 0.7 reduce.15
  135.4 10.4 %all-to-all-done.1 = bf16[16,32,512]{2,1,0:T(8,128)(2,1)} async-done(((bf16[16,32,512]{2,1,0:T(8,128)(2,1)}), bf16[16,32,512]{2,1,0:T(8,128)(2,1)}, u32[]{:S(2)}, u32[]{:S(2)}) %all-to-all-start.1) | async-done | bytes 524320 | tf_op jit(solution)/shard_map/all_to_all | solution.py:94
  145.8 5.5 scatter_custom_fusion.2
  151.3 258.6 %all-reduce.9.cloned.1.call-done = f32[512,512]{1,0:T(8,128)} async-done(((f32[512,512]{1,0:T(8,128)}), f32[512,512]{1,0:T(8,128)}) %all-reduce.9.cloned.1.call-update) | async-done | bytes 1048592 | tf_op jit(solution)/shard_map/psum | solution.py:109
  409.9 2.1 multiply_convert_fusion
  412.0 161.6 %all-reduce.7.cloned.1.call-done = f32[768,512]{1,0:T(8,128)} async-done(((f32[768,512]{1,0:T(8,128)}), f32[768,512]{1,0:T(8,128)}) %all-reduce.7.cloned.1.call-update) | async-done | bytes 1572880 | tf_op jit(solution)/shard_map/psum | solution.py:108
  573.7 2.7 copy.58
  (52 shorter events, 4.1 us)
Async XLA Ops:
  7.2 91.5 %copy-start = (bf16[512,2048]{1,0:T(8,128)(2,1)S(1)}, bf16[512,2048]{1,0:T(8,128)(2,1)}, u32[]{:S(2)}) copy-start(bf16[512,2048]{1,0:T(8,128)(2,1)} %param.11) | copy-start | bytes 6291460
  7.2 83.6 %all-gather.2.cloned.1.call-start = ((), (), s32[]{:S(2)}) async-start(), calls=%async_computation.2 | async-start | bytes 13369344 | tf_op jit(solution)/shard_map/all_gather | solution.py:76
  13.1 111.4 %all-to-all-start = ((s32[16,1,32]{2,1,0:T(1,128)}), s32[16,1,32]{2,1,0:T(1,128)S(1)}, u32[]{:S(2)}, u32[]{:S(2)}) async-start(s32[16,1,32]{2,1,0:T(1,128)} %all_to_all.9), calls=%async_computation | async-start | bytes 16384 | tf_op jit(solution)/shard_map/all_to_all | solution.py:72
  102.4 1.8 copy-start.4
  102.5 1.6 copy-start.6
  102.5 1.6 copy-start.8
  104.1 0.8 copy-start.2
  109.2 2.1 copy-start.5
  109.2 2.3 copy-start.7
  111.2 1.3 copy-start.3
  117.2 4.4 copy-start.1
  124.5 21.3 %all-to-all-start.1 = ((bf16[16,32,512]{2,1,0:T(8,128)(2,1)}), bf16[16,32,512]{2,1,0:T(8,128)(2,1)}, u32[]{:S(2)}, u32[]{:S(2)}) async-start(bf16[16,32,512]{2,1,0:T(8,128)(2,1)} %bitcast.120), calls=%async_computation.1 | async-start | bytes 1048576 | tf_op jit(solution)/shard_map/all_to_all | solution.py:94
  131.4 278.5 %all-reduce.9.cloned.1.call-start = ((), (), s32[]{:S(2)}) async-start(), calls=%async_computation.4 | async-start | bytes 2097152 | tf_op jit(solution)/shard_map/psum | solution.py:109
  134.1 439.6 %all-reduce.7.cloned.1.call-start = ((), (), s32[]{:S(2)}) async-start(), calls=%async_computation.3 | async-start | bytes 3145728 | tf_op jit(solution)/shard_map/psum | solution.py:108
Sparse Core Ops, SparseCore 0:
  10.1 80.5 all-gather.1
  137.3 272.5 all-reduce.8
  414.3 159.3 all-reduce.6
where the time goes:
time: 584 us; the launch traced here: 583 us
  waiting for transfers between devices  498 us (85%)
  local copies, waits for them, and re-layouts  18.5 us (3%)
  other arithmetic  18.5 us (3%)
  starting transfers between devices  17.1 us (3%)
  matrix products  16.5 us (3%)
  between operations  14.6 us (2%)
    psum x1, waiting for transfers between devices, per_device(): dense_total = lax.psum(dense_part, ('dp', 'table'))  259 us
    psum x1, waiting for transfers between devices, per_device(): table_grad = lax.psum(local_grad, 'dp')  162 us
    all_gather x1, waiting for transfers between devices, per_device(): piece = lax.all_gather(table, 'table', axis=0, tiled=True)  66.3 us
  transfers between devices with their start and end apart: 5, of which 4 were waited for; matrix products, arithmetic and copies ran while one was open for 9% of the time, Pallas kernels for 0%

commit v1 on v0

--- a/solution.py
+++ b/solution.py
@@ -73,7 +73,9 @@
         -1
     )
     global_rows = owners * shard_rows + local_rows
-    piece = lax.all_gather(table, "table", axis=0, tiled=True)
+    n_blocks = lax.axis_size("table")
+    spare = jnp.tile(table, [n_blocks if dd == 0 else 1 for dd in range(table.ndim)])
+    piece = lax.all_to_all(spare, concat_axis=0, split_axis=0, tiled=True, axis_name="table")
     inside = (global_rows >= 0) & (global_rows < piece.shape[0])
     taken = piece[jnp.clip(global_rows, 0, piece.shape[0] - 1)].astype(jnp.float32)
     embedded = jnp.where(inside[:, None], taken, 0.0).astype(jnp.bfloat16)

time: 584 us -> 800 us (1.37)
  waiting for transfers between devices: 498 us -> 700 us
    all_to_all x0 -> x1, waiting for transfers between devices: none -> 269 us  [per_device(): lax.all_to_all(spare, concat_axis=0, split_axis=0, tiled=True, axis_name=...]
    all_gather x1 -> x0, waiting for transfers between devices: 66.3 us -> none  [per_device(): piece = lax.all_gather(table, 'table', axis=0, tiled=True)]
    all_to_all x0 -> x1, starting transfers between devices: none -> 10.1 us  [per_device(): lax.all_to_all(spare, concat_axis=0, split_axis=0, tiled=True, axis_name=...]
  transfers between devices with their start and end apart: 5 -> 5, of which waited for: 4 -> 4; matrix products, arithmetic and copies ran while one was open for 9% -> 6% of each run, Pallas kernels for 0% -> 0%
where the time goes in v1:
time: 800 us; the launch traced here: 799 us
  waiting for transfers between devices  700 us (88%)
  local copies, waits for them, and re-layouts  26.2 us (3%)
  starting transfers between devices  23.9 us (3%)
  matrix products  17.5 us (2%)
  other arithmetic  16.5 us (2%)
  between operations  14.9 us (2%)
    all_to_all x1, waiting for transfers between devices, per_device(): lax.all_to_all(spare, concat_axis=0, split_axis=0, tiled=True, axis_name=...  269 us
    psum x1, waiting for transfers between devices, per_device(): dense_total = lax.psum(dense_part, ('dp', 'table'))  259 us
    psum x1, waiting for transfers between devices, per_device(): table_grad = lax.psum(local_grad, 'dp')  162 us
  transfers between devices with their start and end apart: 5, of which 4 were waited for; matrix products, arithmetic and copies ran while one was open for 6% of the time, Pallas kernels for 0%

profile of v1, /device:TPU:64, one launch (start us, length us, event | category | flops | bytes accessed | tf_op | source)
XLA Modules:
  0.0 799.0 jit_solution(3855452248536706553)
XLA Ops:
  7.2 7.0 tile.2
  14.2 10.1 %all-to-all-start.1 = ((bf16[16,768,512]{2,1,0:T(8,128)(2,1)}), bf16[16,768,512]{2,1,0:T(8,128)(2,1)}, u32[]{:S(2)}, u32[]{:S(2)}) async-start(bf16[16,768,512]{2,1,0:T(8,128)(2,1)} %tile.2), calls=%async_computation.1 | async-start | bytes 25165824 | tf_op jit(solution)/shard_map/all_to_all | solution.py:78
  25.2 1.4 scatter_custom_fusion
  26.6 0.7 all_to_all.15
  28.0 269.0 %all-to-all-done.1 = bf16[16,768,512]{2,1,0:T(8,128)(2,1)} async-done(((bf16[16,768,512]{2,1,0:T(8,128)(2,1)}), bf16[16,768,512]{2,1,0:T(8,128)(2,1)}, u32[]{:S(2)}, u32[]{:S(2)}) %all-to-all-start.1) | async-done | bytes 12582944 | tf_op jit(solution)/shard_map/all_to_all | solution.py:78
  297.0 6.2 all-to-all-start
  303.3 7.4 gather_fusion
  311.1 2.8 fusion.76
  314.0 0.8 slice_bitcast_fusion
  315.1 1.6 divide_convert_fusion
  317.7 1.7 multiply_reduce_fusion.1
  319.5 2.1 fusion.75
  321.6 0.8 broadcast_add_fusion
  322.4 1.8 copy.36
  324.2 1.9 fusion.81
  326.1 2.1 fusion.26
  328.6 0.9 fusion.80
  329.5 0.8 copy.39
  330.3 0.8 copy.38
  331.2 1.1 copy.37
  332.3 3.4 multiply_reduce_fusion
  335.7 1.0 fusion.74
  336.7 2.9 scatter_custom_fusion.1
  339.6 7.2 all-to-all-start.2
  346.9 2.5 fusion.45
  350.2 0.7 reduce.15
  350.9 10.4 %all-to-all-done.2 = bf16[16,32,512]{2,1,0:T(8,128)(2,1)} async-done(((bf16[16,32,512]{2,1,0:T(8,128)(2,1)}), bf16[16,32,512]{2,1,0:T(8,128)(2,1)}, u32[]{:S(2)}, u32[]{:S(2)}) %all-to-all-start.2) | async-done | bytes 524320 | tf_op jit(solution)/shard_map/all_to_all | solution.py:96
  361.3 5.5 scatter_custom_fusion.2
  366.8 259.0 %all-reduce.9.cloned.1.call-done = f32[512,512]{1,0:T(8,128)} async-done(((f32[512,512]{1,0:T(8,128)}), f32[512,512]{1,0:T(8,128)}) %all-reduce.9.cloned.1.call-update) | async-done | bytes 1048592 | tf_op jit(solution)/shard_map/psum | solution.py:111
  625.8 2.1 multiply_convert_fusion
  627.9 161.6 %all-reduce.7.cloned.1.call-done = f32[768,512]{1,0:T(8,128)} async-done(((f32[768,512]{1,0:T(8,128)}), f32[768,512]{1,0:T(8,128)}) %all-reduce.7.cloned.1.call-update) | async-done | bytes 1572880 | tf_op jit(solution)/shard_map/psum | solution.py:110
  789.5 2.7 copy.58
  (58 shorter events, 4.1 us)
Async XLA Ops:
  7.2 304.0 %copy-start = (bf16[512,2048]{1,0:T(8,128)(2,1)S(1)}, bf16[512,2048]{1,0:T(8,128)(2,1)}, u32[]{:S(2)}) copy-start(bf16[512,2048]{1,0:T(8,128)(2,1)} %param.11) | copy-start | bytes 6291460
  14.1 10.1 %copy-start.10 = (s32[1,256,1]{1,2,0:T(1,128)S(1)}, s32[1,256,1]{1,2,0:T(1,128)}, u32[]{:S(2)}) copy-start(s32[1,256,1]{1,2,0:T(1,128)} %param.8) | copy-start | bytes 3076
  14.2 11.0 %copy-start.11 = (s32[1,256]{1,0:T(1,128)S(1)}, s32[1,256]{1,0:T(1,128)}, u32[]{:S(2)}) copy-start(s32[1,256]{1,0:T(1,128)} %param.9) | copy-start | bytes 3076
  14.2 282.9 %all-to-all-start.1 = ((bf16[16,768,512]{2,1,0:T(8,128)(2,1)}), bf16[16,768,512]{2,1,0:T(8,128)(2,1)}, u32[]{:S(2)}, u32[]{:S(2)}) async-start(bf16[16,768,512]{2,1,0:T(8,128)(2,1)} %tile.2), calls=%async_computation.1 | async-start | bytes 25165824 | tf_op jit(solution)/shard_map/all_to_all | solution.py:78
  297.0 42.6 %all-to-all-start = ((s32[16,1,32]{2,1,0:T(1,128)}), s32[16,1,32]{2,1,0:T(1,128)S(1)}, u32[]{:S(2)}, u32[]{:S(2)}) async-start(s32[16,1,32]{2,1,0:T(1,128)} %all_to_all.15), calls=%async_computation | async-start | bytes 16384 | tf_op jit(solution)/shard_map/all_to_all | solution.py:72
  314.9 1.7 copy-start.4
  315.0 1.6 copy-start.6
  315.0 1.6 copy-start.9
  316.6 0.8 copy-start.2
  319.4 4.8 copy-start.3
  326.1 2.1 copy-start.7
  326.1 2.4 copy-start.5
  328.2 1.3 copy-start.8
  332.3 4.4 copy-start.1
  339.6 21.7 %all-to-all-start.2 = ((bf16[16,32,512]{2,1,0:T(8,128)(2,1)}), bf16[16,32,512]{2,1,0:T(8,128)(2,1)}, u32[]{:S(2)}, u32[]{:S(2)}) async-start(bf16[16,32,512]{2,1,0:T(8,128)(2,1)} %bitcast.121), calls=%async_computation.2 | async-start | bytes 1048576 | tf_op jit(solution)/shard_map/all_to_all | solution.py:96
  346.8 278.9 %all-reduce.9.cloned.1.call-start = ((), (), s32[]{:S(2)}) async-start(), calls=%async_computation.4 | async-start | bytes 2097152 | tf_op jit(solution)/shard_map/psum | solution.py:111
  349.4 440.1 %all-reduce.7.cloned.1.call-start = ((), (), s32[]{:S(2)}) async-start(), calls=%async_computation.3 | async-start | bytes 3145728 | tf_op jit(solution)/shard_map/psum | solution.py:110
Sparse Core Ops, SparseCore 0:
  352.7 272.9 all-reduce.8
  630.1 159.3 all-reduce.6
